TPU v7x, 512 devices: a whole 4x8x8 slice. The times are simulated.
512 devices in a mesh: interval: 8 (over y), seq: 8 (over x, core), head: 8 (over z).
Axes of the slice: x: 4, y: 8, z: 8, core: 2. Of those that a mesh axis runs over, the one named last changes fastest.
Arguments:
- hidden_in: bfloat16 [8, 2048, 1536], P('interval', 'seq'), may hold values from -6 to 6
- ctx_grad: bfloat16 [8, 2048, 1536], P('interval', 'seq', 'head'), may hold values from -6 to 6
- w_query: bfloat16 [1536, 1536], P('head'), may hold values from -0.15625 to 0.15625
- w_key: bfloat16 [1536, 1536], P('head'), may hold values from -0.15625 to 0.15625
- w_value: bfloat16 [1536, 1536], P('head'), may hold values from -0.15625 to 0.15625
- w_junction: bfloat16 [1536, 128], replicated, may hold values from -0.15625 to 0.15625
- donor_pos: int32 [8, 8, 8, 64], P('interval', 'seq', None, 'head'), may hold values from 0 to 255
- acceptor_pos: int32 [8, 8, 8, 64], P('interval', 'seq', None, 'head'), may hold values from 0 to 255
- junction_counts: int32 [8, 8, 8], P('interval', 'seq'), may hold values from 16 to 64, as said below
- pred_grad: float32 [8, 8, 8, 64], P('interval', 'seq', None, 'head'), may hold values from -6 to 6
Outputs:
- grad_input: bfloat16 [8, 2048, 1536], P('interval', 'seq', 'head')
- grad_query: bfloat16 [1536, 1536], P('head')
- grad_key: bfloat16 [1536, 1536], P('head')
- grad_value: bfloat16 [1536, 1536], P('head')
Inputs may be any that keep to these rules, and one draw needn't show every extreme that they name: `junction_counts`: slots at or past a bucket's count are empty. In each interval one acceptor shard, drawn from the seed, has 64 live slots from every donor shard; every other bucket has 16 to 32.
All inputs are finite; a program needn't handle non-finite values.
Results may differ from a plain program's by a relative error of at most 0.022.
Values may be sent and summed in bfloat16 or wider, within the bound.
No kernel may reach another device: no remote copies, remote signals or barrier semaphores. Data moves between devices by JAX's collectives and lax.ppermute only.
A program may use at most 64 MiB of HBM per device.

v0:
```python
import jax
import jax.numpy as jnp
from jax import lax
from jax.sharding import PartitionSpec as P

HD = 192
PJ = 128


def on_device(
    hidden_in,
    ctx_grad,
    w_query,
    w_key,
    w_value,
    w_junction,
    donor_pos,
    acceptor_pos,
    junction_counts,
    pred_grad,
):
    hidden = hidden_in[0]
    local_len = hidden.shape[0]
    shard_count = lax.axis_size("seq")
    total_len = local_len * shard_count
    heads_dev = w_query.shape[0] // HD
    softmax_scale = HD ** (-0.5)
    pair_scale = PJ ** (-0.5)
    queries = jnp.einsum("td,cd->tc", hidden, w_query, preferred_element_type=jnp.float32).astype(
        jnp.bfloat16
    )
    key_rows = jnp.einsum("td,cd->tc", hidden, w_key, preferred_element_type=jnp.float32).astype(
        jnp.bfloat16
    )
    value_rows = jnp.einsum(
        "td,cd->tc", hidden, w_value, preferred_element_type=jnp.float32
    ).astype(jnp.bfloat16)
    features = jnp.dot(hidden, w_junction, preferred_element_type=jnp.float32).astype(jnp.bfloat16)
    all_keys, all_values, all_features = (
        lax.all_gather(key_rows, "seq", axis=0, tiled=True),
        lax.all_gather(value_rows, "seq", axis=0, tiled=True),
        lax.all_gather(features, "seq", axis=0, tiled=True),
    )
    query_heads = queries.reshape(local_len, heads_dev, HD)
    grad_heads = ctx_grad[0].reshape(local_len, heads_dev, HD)
    key_heads = all_keys.reshape(total_len, heads_dev, HD)
    value_heads = all_values.reshape(total_len, heads_dev, HD)
    scores = (
        jnp.einsum("qhd,khd->hqk", query_heads, key_heads, preferred_element_type=jnp.float32)
        * softmax_scale
    )
    row_max = jnp.max(scores, axis=-1, keepdims=True)
    expd = jnp.exp(scores - row_max)
    probs = expd / jnp.sum(expd, axis=-1, keepdims=True)
    dprobs = jnp.einsum("qhd,khd->hqk", grad_heads, value_heads, preferred_element_type=jnp.float32)
    row_delta = jnp.sum(probs * dprobs, axis=-1, keepdims=True)
    dscores = probs * (dprobs - row_delta)
    probs_b = probs.astype(jnp.bfloat16)
    dscores_b = dscores.astype(jnp.bfloat16)
    query_grad = (
        (
            jnp.einsum("hqk,khd->qhd", dscores_b, key_heads, preferred_element_type=jnp.float32)
            * softmax_scale
        )
        .astype(jnp.bfloat16)
        .reshape(local_len, heads_dev * HD)
    )
    key_term = (
        jnp.einsum("hqk,qhd->khd", dscores_b, query_heads, preferred_element_type=jnp.float32)
        * softmax_scale
    ).reshape(total_len, heads_dev * HD)
    value_term = jnp.einsum(
        "hqk,qhd->khd", probs_b, grad_heads, preferred_element_type=jnp.float32
    ).reshape(total_len, heads_dev * HD)
    key_sum, value_sum = (
        lax.psum_scatter(
            key_term.astype(jnp.bfloat16), "seq", scatter_dimension=0, tiled=True
        ).astype(jnp.float32),
        lax.psum_scatter(
            value_term.astype(jnp.bfloat16), "seq", scatter_dimension=0, tiled=True
        ).astype(jnp.float32),
    )
    key_grad = key_sum.astype(jnp.bfloat16)
    value_grad = value_sum.astype(jnp.bfloat16)
    donor_idx = donor_pos[0, 0]
    accept_idx = acceptor_pos[0, 0]
    slot_dev = donor_idx.shape[1]
    slot_ids = lax.axis_index("head") * slot_dev + jnp.arange(slot_dev, dtype=jnp.int32)
    live_slots = slot_ids[None, :] < junction_counts[0, 0][:, None]
    donor_feat = features[donor_idx].astype(jnp.float32)
    accept_glob = jnp.arange(shard_count, dtype=jnp.int32)[:, None] * local_len + accept_idx
    accept_rows = all_features[accept_glob]
    accept_feat = accept_rows.astype(jnp.float32)
    pair_score = jnp.sum(donor_feat * accept_feat, axis=-1) * pair_scale
    slot_grad = (
        jnp.where(live_slots, pred_grad[0, 0] * jax.nn.sigmoid(pair_score), 0.0) * pair_scale
    )
    donor_term = slot_grad[..., None] * accept_feat
    accept_term = slot_grad[..., None] * donor_feat
    pair_width = features.shape[1]
    grad_feat = (
        jnp.zeros((local_len, pair_width), jnp.float32)
        .at[donor_idx.reshape(-1)]
        .add(donor_term.reshape(-1, pair_width))
    )
    spread_term = (
        jnp.zeros((total_len, pair_width), jnp.float32)
        .at[accept_glob.reshape(-1)]
        .add(accept_term.reshape(-1, pair_width))
    )
    grad_feat = grad_feat + lax.psum_scatter(
        spread_term.astype(jnp.bfloat16), "seq", scatter_dimension=0, tiled=True
    ).astype(jnp.float32)
    grad_feat_b = grad_feat.astype(jnp.bfloat16)
    input_term = jnp.einsum("tc,cd->td", query_grad, w_query, preferred_element_type=jnp.float32)
    input_term = input_term + jnp.einsum(
        "tc,cd->td", key_grad, w_key, preferred_element_type=jnp.float32
    )
    input_term = input_term + jnp.einsum(
        "tc,cd->td", value_grad, w_value, preferred_element_type=jnp.float32
    )
    input_term = input_term + jnp.einsum(
        "tp,dp->td", grad_feat_b, w_junction, preferred_element_type=jnp.float32
    )
    grad_input = lax.psum_scatter(
        input_term.astype(jnp.bfloat16), "head", scatter_dimension=1, tiled=True
    )
    key_wterm = jnp.einsum("tc,td->cd", key_grad, hidden, preferred_element_type=jnp.float32)
    value_wterm = jnp.einsum("tc,td->cd", value_grad, hidden, preferred_element_type=jnp.float32)
    query_wterm = jnp.einsum("tc,td->cd", query_grad, hidden, preferred_element_type=jnp.float32)
    query_wsum, key_wsum, value_wsum = lax.psum(
        (query_wterm, key_wterm, value_wterm), ("interval", "seq")
    )
    return (
        grad_input[None],
        query_wsum.astype(jnp.bfloat16),
        key_wsum.astype(jnp.bfloat16),
        value_wsum.astype(jnp.bfloat16),
    )


def solution(mesh):
    placed = (
        P("interval", "seq", None),
        P("interval", "seq", "head"),
        P("head", None),
        P("head", None),
        P("head", None),
        P(),
        P("interval", "seq", None, "head"),
        P("interval", "seq", None, "head"),
        P("interval", "seq", None),
        P("interval", "seq", None, "head"),
    )
    return jax.shard_map(
        on_device,
        mesh=mesh,
        in_specs=placed,
        out_specs=(P("interval", "seq", "head"), P("head", None), P("head", None), P("head", None)),
        check_vma=False,
    )
```

profile of v0, /device:TPU:64, one launch (start us, length us, event | category | flops | bytes accessed | tf_op | source)
XLA Modules:
  0.0 447.5 jit_solution(17675293737374444175)
XLA Ops:
  7.2 0.8 squeeze.15
  8.1 0.8 compare_select_fusion
  9.0 0.7 compare_select_fusion.1
  9.8 1.3 convolution_convert_fusion.4
  11.1 13.6 %all_gather.11 = bf16[2048,128]{1,0:T(8,128)(2,1)S(1)} all-gather(bf16[256,128]{1,0:T(8,128)(2,1)S(1)} %convolution_convert_fusion.4), channel_id=1, replica_groups=mesh['interval'=8,'seq'=8,'head'=8] {'seq'}, dimensions={0}, use_global_device_ids=true | all-gather | bytes 589824 | tf_op jit(solution)/shard_map/all_gather | solution.py:42
  24.7 0.6 gather_fusion
  25.4 0.8 squeeze.16
  26.3 0.7 lt.67
  27.1 0.6 gather_fusion.1
  27.9 1.1 scatter_custom_fusion
  29.1 0.8 convert_element_type.105
  30.4 13.4 %all_gather.9 = bf16[2048,192]{0,1:T(8,128)(2,1)S(1)} all-gather(bf16[256,192]{0,1:T(8,128)(2,1)S(1)} %convolution_convert_fusion.3), channel_id=1, replica_groups=mesh['interval'=8,'seq'=8,'head'=8] {'seq'}, dimensions={0}, use_global_device_ids=true | all-gather | bytes 884736 | tf_op jit(solution)/shard_map/all_gather | solution.py:40
  44.6 14.2 %all_gather.10 = bf16[2048,192]{1,0:T(8,128)(2,1)S(1)} all-gather(bf16[256,192]{1,0:T(8,128)(2,1)S(1)} %convolution_convert_fusion.1), channel_id=1, replica_groups=mesh['interval'=8,'seq'=8,'head'=8] {'seq'}, dimensions={0}, use_global_device_ids=true | all-gather | bytes 884736 | tf_op jit(solution)/shard_map/all_gather | solution.py:41
  58.8 0.5 fusion.31
  59.8 0.7 multiply_reduce_fusion
  60.5 0.6 multiply_convert_fusion
  61.1 1.0 copy-done.1
  62.1 1.3 fusion.2
  63.5 2.4 convolution_convert_fusion
  66.1 2.0 fusion.6
  68.1 0.5 fusion.32
  68.6 1.5 reduce-scatter.9.cloned.1.call-done
  70.1 0.8 convert_element_type.106
  70.9 1.1 scatter_custom_fusion.1
  72.0 37.1 %reduce-scatter.5.cloned.1.call-done = bf16[256,192]{0,1:T(8,128)(2,1)} async-done(((bf16[2048,192]{0,1:T(8,128)(2,1)}), bf16[256,192]{0,1:T(8,128)(2,1)}) %reduce-scatter.5.cloned.1.call-update) | async-done | bytes 98320 | tf_op jit(solution)/shard_map/reduce_scatter | solution.py:76
  109.1 2.7 convolution_add_fusion.2
  111.8 35.7 %reduce-scatter.7.cloned.1.call-done = bf16[256,192]{0,1:T(8,128)(2,1)} async-done(((bf16[2048,192]{0,1:T(8,128)(2,1)}), bf16[256,192]{0,1:T(8,128)(2,1)}) %reduce-scatter.7.cloned.1.call-update) | async-done | bytes 98320 | tf_op jit(solution)/shard_map/reduce_scatter | solution.py:79
  147.5 1.9 convolution_add_fusion.1
  149.5 1.3 fusion
  151.1 0.5 copy-done.8
  152.0 1.3 fusion.8
  153.3 287.6 %all-reduce.2 = (bf16[192,1536]{1,0:T(8,128)(2,1)}, bf16[192,1536]{1,0:T(8,128)(2,1)}, bf16[192,1536]{1,0:T(8,128)(2,1)}) all-reduce(f32[192,1536]{1,0:T(8,128)S(1)} %fusion.12, f32[192,1536]{1,0:T(8,128)S(1)} %fusion.10, f32[192,1536]{1,0:T(8,128)} %fusion.8), channel_id=1, replica_groups=mesh['interval'=8,'seq'=8,'head'=8] {'interval','seq'}, use_global_device_ids=true, to_apply=%region_10.11 | all-reduce | flops 884736 | bytes 5308416 | tf_op jit(solution)/shard_map/psum | solution.py:131
  (53 shorter events, 3.3 us)
Async XLA Ops:
  7.2 2.6 copy-start
  7.2 62.9 %reduce-scatter.9.cloned.1.call-start = ((), (), s32[]{:S(2)}) async-start(), calls=%async_computation.6 | async-start | bytes 589824 | tf_op jit(solution)/shard_map/reduce_scatter | solution.py:111
  11.1 18.9 %copy-start.4 = (bf16[192,1536]{1,0:T(8,128)(2,1)S(1)}, bf16[192,1536]{1,0:T(8,128)(2,1)}, u32[]{:S(2)}) copy-start(bf16[192,1536]{1,0:T(8,128)(2,1)} %param.13) | copy-start | bytes 1769476
  29.1 14.7 %copy-start.3 = (bf16[192,1536]{1,0:T(8,128)(2,1)S(1)}, bf16[192,1536]{1,0:T(8,128)(2,1)}, u32[]{:S(2)}) copy-start(bf16[192,1536]{1,0:T(8,128)(2,1)} %param.12) | copy-start | bytes 1769476
  29.9 14.3 %copy-start.6 = (bf16[192,1536]{1,0:T(8,128)(2,1)S(1)}, bf16[192,1536]{1,0:T(8,128)(2,1)}, u32[]{:S(2)}) copy-start(bf16[192,1536]{1,0:T(8,128)(2,1)} %param.14) | copy-start | bytes 1769476
  29.9 79.1 %reduce-scatter.5.cloned.1.call-start = ((), (), s32[]{:S(2)}) async-start(), calls=%async_computation.4 | async-start | bytes 884736 | tf_op jit(solution)/shard_map/reduce_scatter | solution.py:76
  43.8 15.0 %copy-start.2 = (bf16[2048,192]{0,1:T(8,128)(2,1)}, bf16[2048,192]{0,1:T(8,128)(2,1)S(1)}, u32[]{:S(2)}) copy-start(bf16[2048,192]{0,1:T(8,128)(2,1)S(1)} %all_gather.9) | copy-start | bytes 2359300
  58.8 1.0 copy-start.11
  61.1 1.0 copy-start.1
  63.5 2.6 copy-start.10
  63.5 84.0 %reduce-scatter.7.cloned.1.call-start = ((), (), s32[]{:S(2)}) async-start(), calls=%async_computation.5 | async-start | bytes 884736 | tf_op jit(solution)/shard_map/reduce_scatter | solution.py:79
  66.0 375.0 %reduce-scatter.11.cloned.1.call-start = ((), (), s32[]{:S(2)}) async-start(), calls=%async_computation.7 | async-start | bytes 884736 | tf_op jit(solution)/shard_map/reduce_scatter | solution.py:125
  68.6 79.0 %copy-start.7 = (bf16[192,1536]{1,0:T(8,128)(2,1)S(1)}, bf16[192,1536]{1,0:T(8,128)(2,1)}, u32[]{:S(2)}) copy-start(bf16[192,1536]{1,0:T(8,128)(2,1)} %param.14) | copy-start | bytes 1769476
  111.8 37.6 %copy-start.5 = (bf16[1536,128]{1,0:T(8,128)(2,1)S(1)}, bf16[1536,128]{1,0:T(8,128)(2,1)}, u32[]{:S(2)}) copy-start(bf16[1536,128]{1,0:T(8,128)(2,1)} %param.15) | copy-start | bytes 1179652
  150.7 0.9 copy-start.8
  150.8 1.2 copy-start.9
Sparse Core Ops, SparseCore 0:
  30.1 39.9 reduce-scatter.8
  73.1 35.9 reduce-scatter.4
  111.9 35.5 reduce-scatter.6
  151.0 39.1 reduce-scatter.10
where the time goes:
time: 448 us; the launch traced here: 447 us
  blocking collectives  329 us (73%)
  waiting for transfers between devices  74.4 us (17%)
  matrix products  17.9 us (4%)
  between operations  14 us (3%)
  other arithmetic  6.55 us (1%)
  local copies, waits for them, and re-layouts  5.71 us (1%)
    psum x1, blocking collectives, on_device(): lax.psum((query_wterm, key_wterm, value_wterm), ('interval', 'seq'))  288 us
    reduce_scatter x1, waiting for transfers between devices, on_device(): lax.psum_scatter(key_term.astype(jnp.bfloat16), 'seq', scatter_dimension=...  37.1 us
    reduce_scatter x1, waiting for transfers between devices, on_device(): lax.psum_scatter(value_term.astype(jnp.bfloat16), 'seq', scatter_dimensio...  35.7 us
    all_gather x1, blocking collectives, on_device(): lax.all_gather(value_rows, 'seq', axis=0, tiled=True)  14.2 us
    all_gather x1, blocking collectives, on_device(): lax.all_gather(features, 'seq', axis=0, tiled=True)  13.6 us
    all_gather x1, blocking collectives, on_device(): lax.all_gather(key_rows, 'seq', axis=0, tiled=True)  13.4 us
  transfers between devices with their start and end apart: 4, of which 3 were waited for; matrix products, arithmetic and copies ran while one was open for 4% of the time, Pallas kernels for 0%

commit v1 on v0

--- a/solution.py
+++ b/solution.py
@@ -128,8 +128,8 @@
     key_wterm = jnp.einsum("tc,td->cd", key_grad, hidden, preferred_element_type=jnp.float32)
     value_wterm = jnp.einsum("tc,td->cd", value_grad, hidden, preferred_element_type=jnp.float32)
     query_wterm = jnp.einsum("tc,td->cd", query_grad, hidden, preferred_element_type=jnp.float32)
-    query_wsum, key_wsum, value_wsum = lax.psum(
-        (query_wterm, key_wterm, value_wterm), ("interval", "seq")
+    query_wsum, key_wsum, value_wsum = jax.lax.psum(
+        jax.lax.psum((query_wterm, key_wterm, value_wterm), "seq"), "interval"
     )
     return (
         grad_input[None],

time: 448 us -> 328 us (0.73)
  the two profiles are of different devices: /device:TPU:64 before, /device:TPU:16 now
where the time goes in v1:
time: 328 us; the launch traced here: 327 us
  waiting for transfers between devices  160 us (49%)
  blocking collectives  119 us (36%)
  matrix products  20.5 us (6%)
  between operations  14.1 us (4%)
  other arithmetic  7.82 us (2%)
  local copies, waits for them, and re-layouts  5.88 us (2%)
    psum x1, blocking collectives, on_device(): jax.lax.psum(jax.lax.psum((query_wterm, key_wterm, value_wterm), 'seq'),...  76.9 us
    psum x1, waiting for transfers between devices, on_device(): jax.lax.psum((query_wterm, key_wterm, value_wterm), 'seq')  76.4 us
    reduce_scatter x1, waiting for transfers between devices, on_device(): lax.psum_scatter(value_term.astype(jnp.bfloat16), 'seq', scatter_dimensio...  36.5 us
    reduce_scatter x1, waiting for transfers between devices, on_device(): lax.psum_scatter(spread_term.astype(jnp.bfloat16), 'seq', scatter_dimensi...  34.2 us
    all_gather x1, blocking collectives, on_device(): lax.all_gather(features, 'seq', axis=0, tiled=True)  14.2 us
    all_gather x1, blocking collectives, on_device(): lax.all_gather(value_rows, 'seq', axis=0, tiled=True)  13.7 us
    all_gather x1, blocking collectives, on_device(): lax.all_gather(key_rows, 'seq', axis=0, tiled=True)  13.7 us
    reduce_scatter x1, waiting for transfers between devices, on_device(): lax.psum_scatter(key_term.astype(jnp.bfloat16), 'seq', scatter_dimension=...  12.9 us
  transfers between devices with their start and end apart: 5, of which 4 were waited for; matrix products, arithmetic and copies ran while one was open for 8% of the time, Pallas kernels for 0%

profile of v1, /device:TPU:16, one launch (start us, length us, event | category | flops | bytes accessed | tf_op | source)
XLA Modules:
  0.0 327.2 jit_solution(11649827562936686372)
XLA Ops:
  7.2 1.1 copy-done
  8.3 1.5 convolution_convert_fusion.3
  9.8 13.7 %all_gather.9 = bf16[2048,192]{0,1:T(8,128)(2,1)S(1)} all-gather(bf16[256,192]{0,1:T(8,128)(2,1)S(1)} %convolution_convert_fusion.3), channel_id=1, replica_groups=mesh['interval'=8,'seq'=8,'head'=8] {'seq'}, dimensions={0}, use_global_device_ids=true | all-gather | bytes 884736 | tf_op jit(solution)/shard_map/all_gather | solution.py:40
  24.3 13.7 %all_gather.10 = bf16[2048,192]{1,0:T(8,128)(2,1)S(1)} all-gather(bf16[256,192]{1,0:T(8,128)(2,1)S(1)} %convolution_convert_fusion.1), channel_id=1, replica_groups=mesh['interval'=8,'seq'=8,'head'=8] {'seq'}, dimensions={0}, use_global_device_ids=true | all-gather | bytes 884736 | tf_op jit(solution)/shard_map/all_gather | solution.py:41
  38.1 0.5 fusion.31
  39.1 0.7 multiply_reduce_fusion
  39.8 0.6 multiply_convert_fusion
  40.4 1.0 copy-done.1
  41.4 1.3 fusion.2
  42.8 2.4 convolution_convert_fusion
  46.2 1.4 convolution_convert_fusion.4
  47.5 0.6 gather_fusion
  48.2 14.2 %all_gather.11 = bf16[2048,128]{1,0:T(8,128)(2,1)} all-gather(bf16[256,128]{1,0:T(8,128)(2,1)S(1)} %convolution_convert_fusion.4), channel_id=1, replica_groups=mesh['interval'=8,'seq'=8,'head'=8] {'seq'}, dimensions={0}, use_global_device_ids=true | all-gather | bytes 589824 | tf_op jit(solution)/shard_map/all_gather | solution.py:42
  62.4 1.7 gather_fusion.1
  64.2 1.9 scatter_custom_fusion
  66.2 2.1 convert_element_type.105
  68.9 0.6 copy-done.8
  69.5 1.3 fusion.12
  70.8 12.9 %reduce-scatter.5.cloned.1.call-done = bf16[256,192]{0,1:T(8,128)(2,1)} async-done(((bf16[2048,192]{0,1:T(8,128)(2,1)}), bf16[256,192]{0,1:T(8,128)(2,1)}) %reduce-scatter.5.cloned.1.call-update) | async-done | bytes 98320 | tf_op jit(solution)/shard_map/reduce_scatter | solution.py:76
  83.7 2.3 fusion.10
  86.0 36.5 %reduce-scatter.7.cloned.1.call-done = bf16[256,192]{0,1:T(8,128)(2,1)} async-done(((bf16[2048,192]{0,1:T(8,128)(2,1)}), bf16[256,192]{0,1:T(8,128)(2,1)}) %reduce-scatter.7.cloned.1.call-update) | async-done | bytes 98320 | tf_op jit(solution)/shard_map/reduce_scatter | solution.py:79
  122.5 2.2 fusion.8
  124.9 0.5 fusion.28
  125.4 1.3 fusion.32
  126.7 34.2 %reduce-scatter.9.cloned.1.call-done = bf16[256,128]{1,0:T(8,128)(2,1)} async-done(((bf16[2048,128]{1,0:T(8,128)(2,1)}), bf16[256,128]{1,0:T(8,128)(2,1)}) %reduce-scatter.9.cloned.1.call-update) | async-done | bytes 65552 | tf_op jit(solution)/shard_map/reduce_scatter | solution.py:111
  161.0 0.8 convert_element_type.106
  161.8 1.2 scatter_custom_fusion.1
  163.0 1.3 convolution_add_fusion.2
  164.4 1.6 convolution_add_fusion.1
  166.0 1.2 fusion
  167.3 76.4 %all-reduce.5.cloned.1.call-done = (f32[192,1536]{1,0:T(8,128)}, f32[192,1536]{1,0:T(8,128)}, f32[192,1536]{1,0:T(8,128)}) async-done(((f32[192,1536]{1,0:T(8,128)}, f32[192,1536]{1,0:T(8,128)}, f32[192,1536]{1,0:T(8,128)}), (f32[192,1536]{1,0:T(8,128)}, f32[192,1536]{1,0:T(8,128)}, f32[192,1536]{1,0:T(8,128)})) %all-reduce.5.cloned.1.call-update) | async-done | bytes 3538960 | tf_op jit(solution)/shard_map/psum | solution.py:132
  243.7 76.9 %all-reduce.6 = (bf16[192,1536]{1,0:T(8,128)(2,1)}, bf16[192,1536]{1,0:T(8,128)(2,1)}, bf16[192,1536]{1,0:T(8,128)(2,1)}) all-reduce(f32[192,1536]{1,0:T(8,128)} %get-tuple-element.4, f32[192,1536]{1,0:T(8,128)} %get-tuple-element.5, f32[192,1536]{1,0:T(8,128)} %get-tuple-element.6), channel_id=1, replica_groups=mesh['interval'=8,'seq'=8,'head'=8] {'interval'}, use_global_device_ids=true, to_apply=%region_11.12 | all-reduce | flops 884736 | bytes 5308416 | tf_op jit(solution)/shard_map/psum | solution.py:131
  (64 shorter events, 3.1 us)
Async XLA Ops:
  7.2 1.1 copy-start
  7.2 16.3 %copy-start.5 = (bf16[192,1536]{1,0:T(8,128)(2,1)S(1)}, bf16[192,1536]{1,0:T(8,128)(2,1)}, u32[]{:S(2)}) copy-start(bf16[192,1536]{1,0:T(8,128)(2,1)} %param.12) | copy-start | bytes 1769476
  7.2 16.7 %copy-start.9 = (bf16[192,1536]{1,0:T(8,128)(2,1)S(1)}, bf16[192,1536]{1,0:T(8,128)(2,1)}, u32[]{:S(2)}) copy-start(bf16[192,1536]{1,0:T(8,128)(2,1)} %param.14) | copy-start | bytes 1769476
  7.2 76.5 %reduce-scatter.5.cloned.1.call-start = ((), (), s32[]{:S(2)}) async-start(), calls=%async_computation.4 | async-start | bytes 884736 | tf_op jit(solution)/shard_map/reduce_scatter | solution.py:76
  23.5 14.6 %copy-start.3 = (bf16[2048,192]{0,1:T(8,128)(2,1)}, bf16[2048,192]{0,1:T(8,128)(2,1)S(1)}, u32[]{:S(2)}) copy-start(bf16[2048,192]{0,1:T(8,128)(2,1)S(1)} %all_gather.9) | copy-start | bytes 2359300
  38.1 1.0 copy-start.15
  40.4 1.0 copy-start.1
  42.7 2.8 copy-start.10
  42.7 2.8 copy-start.11
  42.7 2.9 copy-start.13
  42.7 3.3 copy-start.14
  42.8 79.7 %reduce-scatter.7.cloned.1.call-start = ((), (), s32[]{:S(2)}) async-start(), calls=%async_computation.5 | async-start | bytes 884736 | tf_op jit(solution)/shard_map/reduce_scatter | solution.py:79
  45.3 115.7 %reduce-scatter.9.cloned.1.call-start = ((), (), s32[]{:S(2)}) async-start(), calls=%async_computation.6 | async-start | bytes 589824 | tf_op jit(solution)/shard_map/reduce_scatter | solution.py:111
  47.5 20.8 %copy-start.2 = (bf16[256,2048]{1,0:T(8,128)(2,1)S(1)}, bf16[256,2048]{1,0:T(8,128)(2,1)}, u32[]{:S(2)}) copy-start(bf16[256,2048]{1,0:T(8,128)(2,1)} %copy-done.1) | copy-start | bytes 3145732
  47.5 20.8 %copy-start.4 = (bf16[2048,192]{0,1:T(8,128)(2,1)S(1)}, bf16[2048,192]{0,1:T(8,128)(2,1)}, u32[]{:S(2)}) copy-start(bf16[2048,192]{0,1:T(8,128)(2,1)} %copy-done.3) | copy-start | bytes 2359300
  64.2 4.6 %copy-start.12 = (f32[64]{0:T(128)}, f32[64]{0:T(128)S(1)}, u32[]{:S(2)}) copy-start(f32[64]{0:T(128)S(1)} %fusion.29) | copy-start | bytes 772
  68.3 175.5 %all-reduce.5.cloned.1.call-start = ((), (), s32[]{:S(2)}) async-start(), calls=%async_computation.8 | async-start | bytes 7077888 | tf_op jit(solution)/shard_map/psum | solution.py:132
  68.8 0.6 copy-start.8
  124.7 38.3 %copy-start.6 = (bf16[192,1536]{1,0:T(8,128)(2,1)S(1)}, bf16[192,1536]{1,0:T(8,128)(2,1)}, u32[]{:S(2)}) copy-start(bf16[192,1536]{1,0:T(8,128)(2,1)} %param.13) | copy-start | bytes 1769476
  124.7 195.9 %reduce-scatter.11.cloned.1.call-start = ((), (), s32[]{:S(2)}) async-start(), calls=%async_computation.7 | async-start | bytes 884736 | tf_op jit(solution)/shard_map/reduce_scatter | solution.py:125
  164.4 1.6 copy-start.7
Sparse Core Ops, SparseCore 0:
  42.8 40.8 reduce-scatter.4
  86.8 35.6 reduce-scatter.6
  125.9 35.0 reduce-scatter.8
  163.6 80.1 all-reduce.4
  247.0 41.3 reduce-scatter.10
